TPU v7x, 32 devices: a whole 2x2x4 slice. The times are simulated.
32 devices in a mesh: shard: 2 (over x), ctx: 4 (over z), tp: 4 (over y, core).
Axes of the slice: x: 2, y: 2, z: 4, core: 2. Of those that a mesh axis runs over, the one named last changes fastest.
Arguments:
- hidden_in: bfloat16 [8, 1024, 768], P('shard', 'ctx'), may hold values from -6 to 6
- token_type: int32 [8, 1024], P('shard', 'ctx'), may hold values 0 or 1
- segment: int32 [8, 1024], P('shard', 'ctx'), may hold values from 0 to 17, as said below
- query_weight: bfloat16 [4, 768, 768], P(None, 'shard', 'tp'), may hold values from -0.21875 to 0.21875
- key_value_weight: bfloat16 [2, 768, 768], P(None, 'shard', 'tp'), may hold values from -0.21875 to 0.21875
- query_bias: float32 [4, 768], P(None, 'tp'), may hold values from -1.75 to 1.75
- value_bias: float32 [768], P('tp'), may hold values from -1.75 to 1.75
- out_weight: bfloat16 [768, 768], P('tp', 'shard'), may hold values from -1.75 to 1.75
- out_bias: float32 [768], replicated, may hold values from -1.75 to 1.75
- norm1_gain: float32 [768], replicated, may hold values from 0.5 to 1.5
- norm1_bias: float32 [768], replicated, may hold values from -1.75 to 1.75
- up_weight: bfloat16 [768, 3072], P('shard', 'tp'), may hold values from -0.21875 to 0.21875
- up_bias: float32 [3072], P('tp'), may hold values from -1.75 to 1.75
- down_weight: bfloat16 [3072, 768], P('tp', 'shard'), may hold values from -0.109375 to 0.109375
- down_bias: float32 [768], replicated, may hold values from -1.75 to 1.75
- norm2_gain: float32 [768], replicated, may hold values from 0.5 to 1.5
- norm2_bias: float32 [768], replicated, may hold values from -1.75 to 1.75
- out_grad: bfloat16 [8, 1024, 768], P('shard', 'ctx'), may hold values from -6 to 6
Outputs:
- hidden_out: bfloat16 [8, 1024, 768], P('shard', 'ctx')
- in_grad: float32 [8, 1024, 768], P('shard', 'ctx')
- query_weight_grad: float32 [4, 768, 768], P(None, 'shard', 'tp')
- key_value_weight_grad: float32 [2, 768, 768], P(None, 'shard', 'tp')
- query_bias_grad: float32 [4, 768], P(None, 'tp')
- value_bias_grad: float32 [768], P('tp')
- out_weight_grad: float32 [768, 768], P('tp', 'shard')
- out_bias_grad: float32 [768], replicated
- norm1_gain_grad: float32 [768], replicated
- norm1_bias_grad: float32 [768], replicated
- up_weight_grad: float32 [768, 3072], P('shard', 'tp')
- up_bias_grad: float32 [3072], P('tp')
- down_weight_grad: float32 [3072, 768], P('tp', 'shard')
- down_bias_grad: float32 [768], replicated
- norm2_gain_grad: float32 [768], replicated
- norm2_bias_grad: float32 [768], replicated
Inputs may be any that keep to these rules, and one draw needn't show every extreme that they name: `token_type`: 0 marks a word, 1 an entity. `segment`: within each sequence the documents are numbered 1, 2, 3 in order, each holds 60 to 800 consecutive positions, and the positions after the last document are 0.
All inputs are finite; a program needn't handle non-finite values. No bound on the sum of `token_type` on one device may be relied on, other than what follows from the above.
Results may differ from a plain program's by a relative error of at most 0.02.
Values may be sent and summed in bfloat16 or wider, within the bound.
A program may use at most 128 MiB of HBM per device.

v0:
```python
import jax
import jax.numpy as jnp
from jax import lax
from jax.sharding import PartitionSpec as P

HEAD = 64
FF = 3072
eps_norm = 1e-05
big_neg = -1e30
root_half = 0.7071067811865476
inv_root_two_pi = 0.3989422804014327


def norm_forward(values, gain_vec, bias_vec):
    average = jnp.mean(values, axis=-1, keepdims=True)
    centred = values - average
    variance = jnp.mean(centred * centred, axis=-1, keepdims=True)
    inv_spread = lax.rsqrt(variance + eps_norm)
    normed = centred * inv_spread
    return (normed * gain_vec + bias_vec, normed, inv_spread)


def norm_backward(upstream, normed, inv_spread, gain_vec):
    scaled = upstream * gain_vec
    mean_first = jnp.mean(scaled, axis=-1, keepdims=True)
    second = jnp.mean(scaled * normed, axis=-1, keepdims=True)
    return inv_spread * (scaled - mean_first - normed * second)


def head_scores(queries, key_block, key_word):
    toward_word = jnp.einsum(
        "sqc,skc->sqk", queries[0], key_block, preferred_element_type=jnp.float32
    )
    toward_entity = jnp.einsum(
        "sqc,skc->sqk", queries[1], key_block, preferred_element_type=jnp.float32
    )
    return jnp.where(key_word, toward_word, toward_entity) * HEAD ** (-0.5)


def widen_cols(vector, full_width, offset):
    blank = jnp.zeros(vector.shape[:-1] + (full_width,), jnp.float32)
    return lax.dynamic_update_slice_in_dim(blank, vector, offset, vector.ndim - 1)


def per_device(
    hidden_in,
    token_type,
    segment,
    query_weight,
    key_value_weight,
    query_bias,
    value_bias,
    out_weight,
    out_bias,
    norm1_gain,
    norm1_bias,
    up_weight,
    up_bias,
    down_weight,
    down_bias,
    norm2_gain,
    norm2_bias,
    out_grad,
):
    seq_count, local_len, model_width = hidden_in.shape
    row_count = seq_count * local_len
    tensor_count = lax.axis_size("tp")
    tensor_rank = lax.axis_index("tp")
    share_rows = row_count // tensor_count
    share_start = tensor_rank * share_rows

    def own_rows(values):
        return lax.dynamic_slice_in_dim(values, share_start, share_rows, 0)

    weights_query, weights_keyval, weights_out, weights_up, weights_down = (
        lax.all_gather(query_weight, "shard", axis=1, tiled=True),
        lax.all_gather(key_value_weight, "shard", axis=1, tiled=True),
        lax.all_gather(out_weight, "shard", axis=1, tiled=True),
        lax.all_gather(up_weight, "shard", axis=0, tiled=True),
        lax.all_gather(down_weight, "shard", axis=1, tiled=True),
    )
    part_width = weights_query.shape[2]
    feed_width = weights_up.shape[1]
    heads_here = part_width // HEAD
    row_data = hidden_in.reshape(row_count, model_width)
    is_word = (token_type.reshape(row_count) == 0)[:, None]
    query_four = (
        jnp.einsum("rd,kde->kre", row_data, weights_query, preferred_element_type=jnp.float32)
        + query_bias[:, None, :]
    )
    chosen = jnp.stack(
        [
            jnp.where(is_word, query_four[0], query_four[2]),
            jnp.where(is_word, query_four[1], query_four[3]),
        ]
    ).astype(jnp.bfloat16)
    key_values = jnp.einsum(
        "rd,kde->kre", row_data, weights_keyval, preferred_element_type=jnp.float32
    )
    key_values = (
        key_values + jnp.stack([jnp.zeros_like(value_bias), value_bias])[:, None, :]
    ).astype(jnp.bfloat16)

    def by_head(values):
        return values.reshape(2, seq_count, local_len, heads_here, HEAD).transpose(3, 0, 1, 2, 4)

    def by_rows(values):
        return values.transpose(1, 2, 3, 0, 4).reshape(2, row_count, part_width)

    query_heads = by_head(chosen)
    keys_all = lax.all_gather(by_head(key_values), "ctx", axis=3, tiled=True)
    types_all, segments_all = (
        lax.all_gather(token_type, "ctx", axis=1, tiled=True),
        lax.all_gather(segment, "ctx", axis=1, tiled=True),
    )
    key_word = (types_all == 0)[:, None, :]
    allowed = (segment[:, :, None] == segments_all[:, None, :]) & (segments_all[:, None, :] > 0)

    def attend_head(pieces):
        queries, key_value = pieces
        scores = head_scores(queries, key_value[0], key_word)
        row_max = jnp.max(jnp.where(allowed, scores, big_neg), axis=-1, keepdims=True)
        exponent = jnp.exp(jnp.where(allowed, scores - row_max, big_neg))
        denominator = jnp.maximum(jnp.sum(exponent, axis=-1, keepdims=True), 1.0)
        probability = (exponent / denominator).astype(jnp.bfloat16)
        context = jnp.einsum(
            "sqk,skc->sqc", probability, key_value[1], preferred_element_type=jnp.float32
        )
        return (context.astype(jnp.bfloat16), row_max, denominator)

    context_heads, row_maxima, denominators = lax.map(attend_head, (query_heads, keys_all))
    context = context_heads.transpose(1, 2, 0, 3).reshape(row_count, part_width)
    attn_terms = jnp.dot(context, weights_out, preferred_element_type=jnp.float32)
    grad_output = out_grad.reshape(row_count, model_width).astype(jnp.float32)
    attention = lax.psum(attn_terms.astype(jnp.bfloat16), "tp").astype(jnp.float32) + out_bias
    first_out, first_hat, first_inv = norm_forward(
        row_data.astype(jnp.float32) + attention, norm1_gain, norm1_bias
    )
    first_low = first_out.astype(jnp.bfloat16)
    up_value = jnp.dot(first_low, weights_up, preferred_element_type=jnp.float32) + up_bias
    normal_cdf = 0.5 * (1.0 + lax.erf(up_value * root_half))
    active = jax.nn.gelu(up_value, approximate=False).astype(jnp.bfloat16)
    up_value, normal_cdf, active, down_terms = (
        up_value,
        normal_cdf,
        active,
        jnp.dot(active, weights_down, preferred_element_type=jnp.float32),
    )
    feed_out = lax.psum(down_terms.astype(jnp.bfloat16), "tp").astype(jnp.float32) + down_bias
    final_out, second_hat, second_inv = norm_forward(first_out + feed_out, norm2_gain, norm2_bias)
    hidden_out = final_out.astype(jnp.bfloat16).reshape(seq_count, local_len, model_width)
    grad_second = norm_backward(grad_output, second_hat, second_inv, norm2_gain)
    grad_feed = grad_second.astype(jnp.bfloat16)
    grad_down = jnp.dot(active.T, grad_feed, preferred_element_type=jnp.float32)
    grad_active = jnp.dot(grad_feed, weights_down.T, preferred_element_type=jnp.float32)
    gelu_slope = normal_cdf + up_value * jnp.exp(-0.5 * up_value * up_value) * inv_root_two_pi
    grad_up = (grad_active * gelu_slope).astype(jnp.bfloat16)
    grad_upw = jnp.dot(first_low.T, grad_up, preferred_element_type=jnp.float32)
    up_terms = jnp.dot(grad_up, weights_up.T, preferred_element_type=jnp.float32)
    grad_down, grad_up, grad_upw, up_terms = (grad_down, grad_up, grad_upw, up_terms)
    grad_first = grad_second + lax.psum(up_terms.astype(jnp.bfloat16), "tp").astype(jnp.float32)
    grad_first_in = norm_backward(grad_first, first_hat, first_inv, norm1_gain)
    grad_attention = grad_first_in.astype(jnp.bfloat16)
    first_hat_own, grad_first_own = (own_rows(first_hat), own_rows(grad_first))
    second_hat_own, grad_output_own = (own_rows(second_hat), own_rows(grad_output))
    grad_attn_own, grad_feed_own = (own_rows(grad_attention), own_rows(grad_feed))
    grad_outw = jnp.dot(context.T, grad_attention, preferred_element_type=jnp.float32)
    grad_context = jnp.dot(
        grad_attention, weights_out.T, preferred_element_type=jnp.float32
    ).astype(jnp.bfloat16)
    grad_context_heads = grad_context.reshape(seq_count, local_len, heads_here, HEAD).transpose(
        2, 0, 1, 3
    )

    def attend_back(pieces):
        queries, key_value, grad_ctx_head, row_max, denominator = pieces
        scores = head_scores(queries, key_value[0], key_word)
        probability = jnp.exp(jnp.where(allowed, scores - row_max, big_neg)) / denominator
        grad_weights = jnp.einsum(
            "sqc,skc->sqk", grad_ctx_head, key_value[1], preferred_element_type=jnp.float32
        )
        row_dot = jnp.sum(probability * grad_weights, axis=-1, keepdims=True)
        grad_scores = (probability * (grad_weights - row_dot)).astype(jnp.bfloat16) * jnp.bfloat16(
            HEAD ** (-0.5)
        )
        zero_block = jnp.zeros_like(grad_scores)
        grad_word = jnp.where(key_word, grad_scores, zero_block)
        grad_entity = jnp.where(key_word, zero_block, grad_scores)
        grad_queries = jnp.stack(
            [
                jnp.einsum(
                    "sqk,skc->sqc", grad_word, key_value[0], preferred_element_type=jnp.float32
                ),
                jnp.einsum(
                    "sqk,skc->sqc", grad_entity, key_value[0], preferred_element_type=jnp.float32
                ),
            ]
        )
        grad_keys = jnp.einsum(
            "sqk,sqc->skc", grad_word, queries[0], preferred_element_type=jnp.float32
        )
        grad_keys = grad_keys + jnp.einsum(
            "sqk,sqc->skc", grad_entity, queries[1], preferred_element_type=jnp.float32
        )
        grad_values = jnp.einsum(
            "sqk,sqc->skc",
            probability.astype(jnp.bfloat16),
            grad_ctx_head,
            preferred_element_type=jnp.float32,
        )
        return (grad_queries, jnp.stack([grad_keys, grad_values]))

    grad_query_heads, grad_kv_heads = lax.map(
        attend_back, (query_heads, keys_all, grad_context_heads, row_maxima, denominators)
    )
    grad_kv_mine = lax.psum_scatter(
        grad_kv_heads.astype(jnp.bfloat16), "ctx", scatter_dimension=3, tiled=True
    ).astype(jnp.float32)
    grad_keyval = by_rows(grad_kv_mine).astype(jnp.bfloat16)
    grad_chosen = by_rows(grad_query_heads).astype(jnp.bfloat16)
    zero_rows = jnp.zeros_like(grad_chosen[0])
    grad_query_four = jnp.stack(
        [
            jnp.where(is_word, grad_chosen[0], zero_rows),
            jnp.where(is_word, grad_chosen[1], zero_rows),
            jnp.where(is_word, zero_rows, grad_chosen[0]),
            jnp.where(is_word, zero_rows, grad_chosen[1]),
        ]
    )
    grad_queryw = jnp.einsum(
        "rd,kre->kde", row_data, grad_query_four, preferred_element_type=jnp.float32
    )
    grad_keyvalw = jnp.einsum(
        "rd,kre->kde", row_data, grad_keyval, preferred_element_type=jnp.float32
    )
    back_input = jnp.einsum(
        "kre,kde->rd", grad_query_four, weights_query, preferred_element_type=jnp.float32
    )
    back_input = back_input + jnp.einsum(
        "kre,kde->rd", grad_keyval, weights_keyval, preferred_element_type=jnp.float32
    )
    in_grad = (
        grad_first_in + lax.psum(back_input.astype(jnp.bfloat16), "tp").astype(jnp.float32)
    ).reshape(seq_count, local_len, model_width)
    column_at = tensor_rank * part_width
    feed_at = tensor_rank * feed_width
    small_grads = lax.psum(
        (
            jnp.sum(grad_first_own * first_hat_own, axis=0),
            jnp.sum(grad_first_own, axis=0),
            jnp.sum(grad_output_own * second_hat_own, axis=0),
            jnp.sum(grad_output_own, axis=0),
            jnp.sum(grad_attn_own, axis=0, dtype=jnp.float32),
            jnp.sum(grad_feed_own, axis=0, dtype=jnp.float32),
            widen_cols(jnp.sum(grad_query_four, axis=1, dtype=jnp.float32), model_width, column_at),
            widen_cols(jnp.sum(grad_keyval[1], axis=0, dtype=jnp.float32), model_width, column_at),
            widen_cols(jnp.sum(grad_up, axis=0, dtype=jnp.float32), FF, feed_at),
        ),
        ("shard", "ctx", "tp"),
    )
    (
        gain_one_grad,
        shift_one_grad,
        gain_two_grad,
        shift_two_grad,
        out_shift_grad,
        down_shift_grad,
        query_full,
        value_full,
        up_full,
    ) = small_grads
    query_shift_grad = lax.dynamic_slice_in_dim(query_full, column_at, part_width, 1)
    value_shift_grad = lax.dynamic_slice_in_dim(value_full, column_at, part_width, 0)
    up_shift_grad = lax.dynamic_slice_in_dim(up_full, feed_at, feed_width, 0)
    weight_grads = (grad_queryw, grad_keyvalw, grad_outw, grad_upw, grad_down)
    summed = (
        lax.psum(weight_grads[0].astype(jnp.bfloat16), "ctx").astype(jnp.float32),
        lax.psum(weight_grads[1].astype(jnp.bfloat16), "ctx").astype(jnp.float32),
        lax.psum(weight_grads[2].astype(jnp.bfloat16), "ctx").astype(jnp.float32),
        lax.psum(weight_grads[3].astype(jnp.bfloat16), "ctx").astype(jnp.float32),
        lax.psum(weight_grads[4].astype(jnp.bfloat16), "ctx").astype(jnp.float32),
    )
    my_grads = (
        lax.psum_scatter(
            summed[0].astype(jnp.bfloat16), "shard", scatter_dimension=1, tiled=True
        ).astype(jnp.float32),
        lax.psum_scatter(
            summed[1].astype(jnp.bfloat16), "shard", scatter_dimension=1, tiled=True
        ).astype(jnp.float32),
        lax.psum_scatter(
            summed[2].astype(jnp.bfloat16), "shard", scatter_dimension=1, tiled=True
        ).astype(jnp.float32),
        lax.psum_scatter(
            summed[3].astype(jnp.bfloat16), "shard", scatter_dimension=0, tiled=True
        ).astype(jnp.float32),
        lax.psum_scatter(
            summed[4].astype(jnp.bfloat16), "shard", scatter_dimension=1, tiled=True
        ).astype(jnp.float32),
    )
    return (
        hidden_out,
        in_grad,
        my_grads[0],
        my_grads[1],
        query_shift_grad,
        value_shift_grad,
        my_grads[2],
        out_shift_grad,
        gain_one_grad,
        shift_one_grad,
        my_grads[3],
        up_shift_grad,
        my_grads[4],
        down_shift_grad,
        gain_two_grad,
        shift_two_grad,
    )


def solution(mesh):
    in_specs = (
        P("shard", "ctx", None),
        P("shard", "ctx"),
        P("shard", "ctx"),
        P(None, "shard", "tp"),
        P(None, "shard", "tp"),
        P(None, "tp"),
        P("tp"),
        P("tp", "shard"),
        P(),
        P(),
        P(),
        P("shard", "tp"),
        P("tp"),
        P("tp", "shard"),
        P(),
        P(),
        P(),
        P("shard", "ctx", None),
    )
    out_specs = (
        P("shard", "ctx", None),
        P("shard", "ctx", None),
        P(None, "shard", "tp"),
        P(None, "shard", "tp"),
        P(None, "tp"),
        P("tp"),
        P("tp", "shard"),
        P(),
        P(),
        P(),
        P("shard", "tp"),
        P("tp"),
        P("tp", "shard"),
        P(),
        P(),
        P(),
    )
    return jax.shard_map(
        per_device, mesh=mesh, in_specs=in_specs, out_specs=out_specs, check_vma=False
    )
```

profile of v0, /device:TPU:0, one launch (start us, length us, event | category | flops | bytes accessed | tf_op | source)
XLA Modules:
  0.0 815.5 jit_solution(1495779303078105990)
XLA Ops:
  8.6 10.9 %all_gather.26 = bf16[2,768,192]{1,2,0:T(8,128)(2,1)S(1)} all-gather(bf16[2,384,192]{1,2,0:T(8,128)(2,1)} %param.26), channel_id=1, replica_groups=mesh['shard'=2,'ctx'=4,'tp'=4] {'shard'}, dimensions={1}, use_global_device_ids=true | all-gather | bytes 884736 | tf_op jit(solution)/shard_map/all_gather | solution.py:77
  24.4 13.6 %all_gather.24 = s32[4,1024]{1,0:T(4,128)S(1)} all-gather(s32[4,256]{1,0:T(4,128)S(1)} %copy-done.43), channel_id=1, replica_groups=mesh['shard'=2,'ctx'=4,'tp'=4] {'ctx'}, dimensions={1}, use_global_device_ids=true | all-gather | bytes 20480 | tf_op jit(solution)/shard_map/all_gather | solution.py:113
  38.1 13.3 %all_gather.28 = s32[4,1024]{1,0:T(4,128)S(1)} all-gather(s32[4,256]{1,0:T(4,128)S(1)} %copy-done.22), channel_id=1, replica_groups=mesh['shard'=2,'ctx'=4,'tp'=4] {'ctx'}, dimensions={1}, use_global_device_ids=true | all-gather | bytes 20480 | tf_op jit(solution)/shard_map/all_gather | solution.py:114
  51.3 5.9 all_gather.29
  58.4 2.7 add_bitcast_fusion
  64.9 35.8 %all-gather.7.cloned.1.call-done = bf16[3,2,4,1024,64]{3,4,2,1,0:T(8,128)(2,1)} async-done(((bf16[3,2,4,256,64]{3,4,2,1,0:T(8,128)(2,1)}), bf16[3,2,4,1024,64]{3,4,2,1,0:T(8,128)(2,1)}) %all-gather.7.cloned.1.call-update) | async-done | bytes 3145744 | tf_op jit(solution)/shard_map/all_gather | solution.py:111
  100.7 30.9 %while.28 = (s32[]{:T(128)}, bf16[3,4,256,64]{2,3,1,0:T(8,128)(2,1)}, f32[3,4,256,1]{2,1,3,0:T(4,128)}, f32[3,4,256,1]{2,1,3,0:T(4,128)}, pred[4,1,1024]{2,0,1:T...) while((s32[]{:T(128)}, ...), condition=%wide.region_3.4_spmd.clone, body=%wide.region_0.3_spmd.clone.sunk | while | flops 420544512 | bytes 23113960 | solution.py:131
  102.5 2.8 select_reduce_fusion.2
  107.1 3.3 fusion.170
  112.8 2.8 select_reduce_fusion.2
  117.4 3.3 fusion.170
  123.1 2.8 select_reduce_fusion.2
  127.7 3.3 fusion.170
  136.4 39.8 %all-reduce.9.cloned.1.call-done = bf16[1024,768]{1,0:T(8,128)(2,1)} async-done(((bf16[1024,768]{1,0:T(8,128)(2,1)}), bf16[1024,768]{1,0:T(8,128)(2,1)}) %all-reduce.9.cloned.1.call-update) | async-done | bytes 1572880 | tf_op jit(solution)/shard_map/psum | solution.py:135
  181.4 19.1 %all-gather.9.cloned.1.call-done = bf16[768,768]{1,0:T(8,128)(2,1)} async-done(((bf16[384,768]{1,0:T(8,128)(2,1)}), bf16[768,768]{1,0:T(8,128)(2,1)}) %all-gather.9.cloned.1.call-update) | async-done | bytes 1179664 | tf_op jit(solution)/shard_map/all_gather | solution.py:79
  200.5 10.3 %fusion.93 = (bf16[1024,768]{1,0:T(8,128)(2,1)}, f32[1024,768]{1,0:T(8,128)}) fusion(f32[768]{0:T(1024)S(1)} %copy-done.50, bf16[768,768]{1,0:T(8,128)(2,1)} %all-gather.9.cloned.1.call-done, f32[1024,768]{1,0:T(8,128)S(1)} %subtract_multiply_fusion.3, f32[768]{0:T(1024)S(1)} %copy-done.36, f32[768]{0:T(1024)S(1)} %copy-done.29), kind=kOutput, calls=%fused_computation.90 | convolution fusion | flops 1262223360 | bytes 9053184 | tf_op jit(solution)/shard_map/dot_general | solution.py:140
  210.7 13.9 %all-gather.11.cloned.1.call-done = bf16[768,768]{1,0:T(8,128)(2,1)} async-done(((bf16[768,384]{1,0:T(8,128)(2,1)}), bf16[768,768]{1,0:T(8,128)(2,1)}) %all-gather.11.cloned.1.call-update) | async-done | bytes 1179664 | tf_op jit(solution)/shard_map/all_gather | solution.py:80
  224.6 4.3 convolution_convert_fusion.1
  230.8 41.1 %all-reduce.11.cloned.1.call-done = bf16[1024,768]{1,0:T(8,128)(2,1)} async-done(((bf16[1024,768]{1,0:T(8,128)(2,1)}), bf16[1024,768]{1,0:T(8,128)(2,1)}) %all-reduce.11.cloned.1.call-update) | async-done | bytes 1572880 | tf_op jit(solution)/shard_map/psum | solution.py:149
  281.3 3.4 convert_reduce_fusion
  288.7 42.8 %all-reduce.13.cloned.1.call-done = bf16[1024,768]{1,0:T(8,128)(2,1)} async-done(((bf16[1024,768]{1,0:T(8,128)(2,1)}), bf16[1024,768]{1,0:T(8,128)(2,1)}) %all-reduce.13.cloned.1.call-update) | async-done | bytes 1572880 | tf_op jit(solution)/shard_map/psum | solution.py:161
  331.5 4.8 multiply_reduce_fusion.6
  343.8 150.3 %while.29 = (s32[]{:T(128)}, bf16[3,2,4,256,64]{3,4,2,1,0:T(8,128)(2,1)}, bf16[3,2,4,1024,64]{3,4,2,1,0:T(8,128)(2,1)}, pred[4,1,1024]{2,0,1:T(4,128)(4,1)}, bf1...) while((s32[]{:T(128)}, ...), condition=%wide.region_17.18_spmd.clone, body=%wide.region_15.17_spmd.clone.sunk | while | flops 1123033088 | bytes 97640736 | solution.py:213
  344.5 3.8 fusion.179
  350.1 5.1 exponential_divide_fusion.2
  355.2 7.7 fusion.181
  362.9 7.7 fusion.180
  372.3 3.5 fusion.183
  375.8 7.9 fusion.184
  383.7 8.0 fusion.185
  394.6 3.8 fusion.179
  400.2 5.0 exponential_divide_fusion.2
  405.3 7.7 fusion.181
  413.0 7.7 fusion.180
  422.4 3.5 fusion.183
  425.9 7.9 fusion.184
  433.8 8.0 fusion.185
  444.7 3.8 fusion.179
  450.3 5.0 exponential_divide_fusion.2
  455.4 7.7 fusion.181
  463.1 7.7 fusion.180
  472.5 3.5 fusion.183
  476.0 7.9 fusion.184
  483.8 8.0 fusion.185
  500.0 4.6 convolution_convert_fusion.3
  514.9 3.8 fusion.110
  518.7 3.6 copy.56
  522.3 4.0 reshape.227
  526.4 28.3 %reduce-scatter.15.cloned.1.call-done = bf16[3,2,4,256,64]{3,4,2,1,0:T(8,128)(2,1)} async-done(((bf16[3,2,4,1024,64]{3,4,2,1,0:T(8,128)(2,1)}), bf16[3,2,4,256,64]{3,4,2,1,0:T(8,128)(2,1)}) %reduce-scatter.15.cloned.1.call-update) | async-done | bytes 786448 | tf_op jit(solution)/shard_map/reduce_scatter | solution.py:216
  554.7 2.6 copy.55
  559.9 3.3 fusion.112
  563.1 3.0 copy.58
  566.1 3.0 reshape.229
  569.2 3.9 convolution_convert_fusion.4
  573.4 3.2 fusion.120
  580.6 14.0 %reduce-scatter.25.cloned.1.call-done = bf16[384,768]{1,0:T(8,128)(2,1)} async-done(((bf16[768,768]{1,0:T(8,128)(2,1)}), bf16[384,768]{1,0:T(8,128)(2,1)}) %reduce-scatter.25.cloned.1.call-update) | async-done | bytes 589840
  596.7 22.6 %reduce-scatter.19.cloned.1.call-done = bf16[384,768]{1,0:T(8,128)(2,1)} async-done(((bf16[768,768]{1,0:T(8,128)(2,1)}), bf16[384,768]{1,0:T(8,128)(2,1)}) %reduce-scatter.19.cloned.1.call-update) | async-done | bytes 589840
  619.3 2.9 reshape.228
  624.3 12.5 %reduce-scatter.21.cloned.1.call-done = bf16[384,384]{1,0:T(8,128)(2,1)} async-done(((bf16[768,384]{1,0:T(8,128)(2,1)}), bf16[384,384]{1,0:T(8,128)(2,1)}) %reduce-scatter.21.cloned.1.call-update) | async-done | bytes 294928
  639.3 22.2 %reduce-scatter.17.cloned.1.call-done = bf16[384,768]{1,0:T(8,128)(2,1)} async-done(((bf16[768,768]{1,0:T(8,128)(2,1)}), bf16[384,768]{1,0:T(8,128)(2,1)}) %reduce-scatter.17.cloned.1.call-update) | async-done | bytes 589840 | tf_op jit(solution)/shard_map/reduce_scatter | solution.py:293
  661.5 3.4 bitcast_convert_fusion
  675.8 41.3 %all-reduce.1 = (f32[4,768]{1,0:T(4,128)S(1)}, f32[768]{0:T(1024)S(1)}, f32[768]{0:T(1024)}, f32[768]{0:T(1024)}, f32[768]{0:T(1024)}, /*index=5*/f32[3072]{0:T(...) all-reduce(f32[4,768]{1,0:T(4,128)S(1)} %dynamic_update_slice.28, ...), channel_id=1, replica_groups=mesh['shard'=2,'ctx'=4,'tp'=4] {'shard','ctx','tp'}, use_global_device_ids=true, to_apply=%region_25.26 | all-reduce | flops 11520 | bytes 92160 | tf_op jit(solution)/shard_map/psum | solution.py:247
  719.1 4.1 convert_add_fusion
  723.2 77.6 %all-reduce.17.cloned.1.call-done = (bf16[4,384,192]{1,2,0:T(8,128)(2,1)}, bf16[2,384,192]{1,2,0:T(8,128)(2,1)}, bf16[192,384]{1,0:T(8,128)(2,1)}, bf16[384,768]{1,0:T(8,128)(2,1)}, bf16[768,384]{1,0:T(8,128)(2,1)}) async-done(((bf16[4,384,192]{1,2,0:T(8,128)(2,1)}, bf16[2,384,192]{1,2,0:T(8,128)(2,1)}, bf16[192,384]{1,0:T(8,128)(2,1)}, bf16[384,768]{1,0:T(8,128)(2,1)}, bf16[768,384]{1,0:T(8,128)(2,1)}), ...) | async-done | bytes 2211856 | tf_op jit(solution)/shard_map/psum | solution.py:277
  (266 shorter events, 126.1 us)
Async XLA Ops:
  7.2 51.2 %all-gather.5.cloned.1.call-start = ((), (), s32[]{:S(2)}) async-start(), calls=%async_computation.6 | async-start | bytes 1769472 | tf_op jit(solution)/shard_map/all_gather | solution.py:76
  7.9 92.7 %all-gather.7.cloned.1.call-start = ((), (), s32[]{:S(2)}) async-start(), calls=%async_computation.7 | async-start | bytes 3932160 | tf_op jit(solution)/shard_map/all_gather | solution.py:111
  20.4 4.0 copy-start.43
  20.4 17.7 %copy-start.22 = (s32[4,256]{1,0:T(4,128)S(1)}, s32[4,256]{1,0:T(4,128)}, u32[]{:S(2)}) copy-start(s32[4,256]{1,0:T(4,128)} %param.24) | copy-start | bytes 12292
  20.4 31.0 %copy-start.31 = (bf16[192,384]{1,0:T(8,128)(2,1)S(1)}, bf16[192,384]{1,0:T(8,128)(2,1)}, u32[]{:S(2)}) copy-start(bf16[192,384]{1,0:T(8,128)(2,1)} %param.29) | copy-start | bytes 442372
  22.6 35.8 %copy-start.3 = (bf16[4,256,768]{2,1,0:T(8,128)(2,1)S(1)}, bf16[4,256,768]{2,1,0:T(8,128)(2,1)}, u32[]{:S(2)}) copy-start(bf16[4,256,768]{2,1,0:T(8,128)(2,1)} %param.22) | copy-start | bytes 4718596
  22.7 35.8 %copy-start.49 = (f32[4,192]{1,0:T(4,128)S(1)}, f32[4,192]{1,0:T(4,128)}, u32[]{:S(2)}) copy-start(f32[4,192]{1,0:T(4,128)} %param.27) | copy-start | bytes 9220
  24.3 151.9 %all-reduce.9.cloned.1.call-start = ((), (), s32[]{:S(2)}) async-start(), calls=%async_computation.8 | async-start | bytes 3145728 | tf_op jit(solution)/shard_map/psum | solution.py:135
  24.4 36.7 %copy-start.44 = (pred[1024]{0:T(1024)(128)(4,1)}, pred[1024]{0:T(1024)(128)(4,1)S(1)}, u32[]{:S(2)}) copy-start(pred[1024]{0:T(1024)(128)(4,1)S(1)} %eq.36) | copy-start | bytes 3076
  100.7 32.6 %copy-start.19 = (bf16[192,768]{1,0:T(8,128)(2,1)S(1)}, bf16[192,768]{1,0:T(8,128)(2,1)}, u32[]{:S(2)}) copy-start(bf16[192,768]{1,0:T(8,128)(2,1)} %all_gather.29) | copy-start | bytes 884740
  100.7 1.8 copy-start.23
  100.7 1.9 copy-start.25
  100.7 1.9 copy-start.27
  111.0 1.9 copy-start.27
  121.3 1.8 copy-start.27
  131.5 4.7 copy-start.6
  131.5 44.7 %copy-start.42 = (f32[768]{0:T(1024)S(1)}, f32[768]{0:T(1024)}, u32[]{:S(2)}) copy-start(f32[768]{0:T(1024)} %param.30) | copy-start | bytes 9220
  133.2 45.1 %copy-start.8 = (bf16[24,8,4,256]{3,1,2,0:T(8,128)(2,1)}, bf16[24,8,4,256]{3,1,2,0:T(8,128)(2,1)S(1)}, u32[]{:S(2)}) copy-start(bf16[24,8,4,256]{3,1,2,0:T(8,128)(2,1)S(1)} %copy.64) | copy-start | bytes 1179652
  135.0 65.4 %all-gather.9.cloned.1.call-start = ((), (), s32[]{:S(2)}) async-start(), calls=%async_computation.9 | async-start | bytes 1769472 | tf_op jit(solution)/shard_map/all_gather | solution.py:79
  135.6 89.0 %all-gather.11.cloned.1.call-start = ((), (), s32[]{:S(2)}) async-start(), calls=%async_computation.10 | async-start | bytes 1769472 | tf_op jit(solution)/shard_map/all_gather | solution.py:80
  136.2 135.8 %all-reduce.11.cloned.1.call-start = ((), (), s32[]{:S(2)}) async-start(), calls=%async_computation.11 | async-start | bytes 3145728 | tf_op jit(solution)/shard_map/psum | solution.py:149
  176.2 2.1 copy-start.4
  179.3 157.1 %copy-start.33 = (f32[1024]{0:T(1024)}, f32[1024]{0:T(1024)S(1)}, u32[]{:S(2)}) copy-start(f32[1024]{0:T(1024)S(1)} %add_rsqrt_fusion.1) | copy-start | bytes 12292
  179.3 21.2 %copy-start.29 = (f32[768]{0:T(1024)S(1)}, f32[768]{0:T(1024)}, u32[]{:S(2)}) copy-start(f32[768]{0:T(1024)} %param.31) | copy-start | bytes 9220
  179.3 21.2 %copy-start.36 = (f32[768]{0:T(1024)S(1)}, f32[768]{0:T(1024)}, u32[]{:S(2)}) copy-start(f32[768]{0:T(1024)} %param.32) | copy-start | bytes 9220
  179.3 21.2 %copy-start.50 = (f32[768]{0:T(1024)S(1)}, f32[768]{0:T(1024)}, u32[]{:S(2)}) copy-start(f32[768]{0:T(1024)} %param.34) | copy-start | bytes 9220
  224.6 4.4 copy-start.32
  228.9 43.0 %copy-start.35 = (f32[768]{0:T(1024)S(1)}, f32[768]{0:T(1024)}, u32[]{:S(2)}) copy-start(f32[768]{0:T(1024)} %param.36) | copy-start | bytes 9220
  229.0 102.6 %all-reduce.13.cloned.1.call-start = ((), (), s32[]{:S(2)}) async-start(), calls=%async_computation.12 | async-start | bytes 3145728 | tf_op jit(solution)/shard_map/psum | solution.py:161
  272.0 2.2 copy-start.5
  277.3 2.2 copy-start.48
  277.3 3.9 copy-start.52
  279.0 5.6 copy-start.11
  281.3 4.6 copy-start.47
  285.9 45.7 %copy-start.46 = (f32[768]{0:T(1024)S(1)}, f32[768]{0:T(1024)}, u32[]{:S(2)}) copy-start(f32[768]{0:T(1024)} %param.38) | copy-start | bytes 9220
  288.5 266.2 %reduce-scatter.15.cloned.1.call-start = ((), (), s32[]{:S(2)}) async-start(), calls=%async_computation.13 | async-start | bytes 3932160 | tf_op jit(solution)/shard_map/reduce_scatter | solution.py:216
  348.2 1.9 copy-start.24
  348.2 1.9 copy-start.26
  348.2 1.9 copy-start.28
  398.3 1.9 copy-start.24
  398.3 1.9 copy-start.26
  398.3 1.9 copy-start.28
  448.4 1.9 copy-start.24
  448.4 1.9 copy-start.26
  448.4 1.9 copy-start.28
  494.1 84.8 %reduce-scatter.23.cloned.1.call-start = ((), (), s32[]{:S(2)}) async-start(), calls=%async_computation.18 | async-start | bytes 589824
  499.6 95.0 %reduce-scatter.25.cloned.1.call-start = ((), (), s32[]{:S(2)}) async-start(), calls=%async_computation.19 | async-start | bytes 1769472
  507.0 5.7 copy-start.45
  507.0 112.3 %reduce-scatter.19.cloned.1.call-start = ((), (), s32[]{:S(2)}) async-start(), calls=%async_computation.16 | async-start | bytes 1769472
  513.9 59.5 %copy-start.14 = (bf16[1,1024,192]{1,2,0:T(8,128)(2,1)}, bf16[1,1024,192]{1,2,0:T(8,128)(2,1)S(1)}, u32[]{:S(2)}) copy-start(bf16[1,1024,192]{1,2,0:T(8,128)(2,1)S(1)} %get-tuple-element.250) | copy-start | bytes 1179652
  526.3 110.5 %reduce-scatter.21.cloned.1.call-start = ((), (), s32[]{:S(2)}) async-start(), calls=%async_computation.17 | async-start | bytes 884736
  559.8 9.4 %copy-start.30 = (f32[768]{0:T(1024)S(1)}, f32[768]{0:T(1024)}, u32[]{:S(2)}) copy-start(f32[768]{0:T(1024)} %param.31) | copy-start | bytes 9220
  559.8 9.4 %copy-start.37 = (f32[768]{0:T(1024)S(1)}, f32[768]{0:T(1024)}, u32[]{:S(2)}) copy-start(f32[768]{0:T(1024)} %param.32) | copy-start | bytes 9220
  569.1 92.3 %reduce-scatter.17.cloned.1.call-start = ((), (), s32[]{:S(2)}) async-start(), calls=%async_computation.15 | async-start | bytes 1769472 | tf_op jit(solution)/shard_map/reduce_scatter | solution.py:293
  573.1 146.0 %all-reduce.15.cloned.1.call-start = ((), (), s32[]{:S(2)}) async-start(), calls=%async_computation.14 | async-start | bytes 3145728 | tf_op jit(solution)/shard_map/psum | solution.py:243
  573.4 3.2 copy-start.10
  573.4 3.2 copy-start.13
  578.8 222.0 %all-reduce.17.cloned.1.call-start = ((), (), s32[]{:S(2)}) async-start(), calls=%async_computation.20 | async-start | bytes 4423680 | tf_op jit(solution)/shard_map/psum | solution.py:277
  661.5 7.6 copy-start.15
  664.9 54.2 %copy-start.34 = (f32[1024]{0:T(1024)S(1)}, f32[1024]{0:T(1024)}, u32[]{:S(2)}) copy-start(f32[1024]{0:T(1024)} %copy-done.33) | copy-start | bytes 12292
  664.9 54.2 %copy-start.39 = (f32[1024]{0:T(1024)S(1)}, f32[1024]{0:T(1024)}, u32[]{:S(2)}) copy-start(f32[1024]{0:T(1024)} %copy-done.38) | copy-start | bytes 12292
  664.9 54.2 %copy-start.41 = (f32[1024]{0:T(1024)S(1)}, f32[1024]{0:T(1024)}, u32[]{:S(2)}) copy-start(f32[1024]{0:T(1024)} %copy-done.40) | copy-start | bytes 12292
  800.8 5.7 copy-start.21
  800.8 6.8 copy-start.20
  (16 other events, 22.4 us)
Sparse Core Ops, SparseCore 0:
  9.5 25.4 all-gather.4
  37.2 63.4 all-gather.6
  135.1 41.0 all-reduce.8
  177.6 22.7 all-gather.8
  201.8 22.7 all-gather.10
  229.1 42.8 all-reduce.10
  288.6 42.9 all-reduce.12
  494.2 60.4 reduce-scatter.14
  556.9 13.0 reduce-scatter.22
  572.7 21.8 reduce-scatter.24
  597.4 21.8 reduce-scatter.18
  621.4 15.3 reduce-scatter.20
  639.6 21.8 reduce-scatter.16
  663.7 43.4 all-reduce.14
  710.4 90.3 all-reduce.16
where the time goes:
time: 824 us; the launch traced here: 815 us
  waiting for transfers between devices  372 us (45%)
  matrix products  212 us (26%)
  blocking collectives  85 us (10%)
  local copies, waits for them, and re-layouts  66 us (8%)
  other arithmetic  64.1 us (8%)
  between operations  14.7 us (2%)
    psum x1, waiting for transfers between devices, per_device(): lax.psum(weight_grads[0].astype(jnp.bfloat16), 'ctx').astype(jnp.float32)  77.6 us
    unnamed x19, waiting for transfers between devices  51 us
    psum x1, waiting for transfers between devices, per_device(): lax.psum(up_terms.astype(jnp.bfloat16), 'tp').astype(jnp.float32)  42.8 us
    psum x1, blocking collectives, per_device(): lax.psum((jnp.sum(grad_first_own * first_hat_own, axis=0), jnp.sum(grad_f...  41.3 us
    psum x1, waiting for transfers between devices, per_device(): lax.psum(down_terms.astype(jnp.bfloat16), 'tp').astype(jnp.float32)  41.1 us
    psum x1, waiting for transfers between devices, per_device(): lax.psum(attn_terms.astype(jnp.bfloat16), 'tp').astype(jnp.float32)  39.8 us
    unnamed x108, local copies, waits for them, and re-layouts  38.4 us
    all_gather x1, waiting for transfers between devices, per_device(): keys_all = lax.all_gather(by_head(key_values), 'ctx', axis=3, tiled=True)  35.8 us
  transfers between devices with their start and end apart: 15, of which 12 were waited for; matrix products, arithmetic and copies ran while one was open for 14% of the time, Pallas kernels for 0%

commit v1 on v0

--- a/solution.py
+++ b/solution.py
@@ -274,7 +274,9 @@
     up_shift_grad = lax.dynamic_slice_in_dim(up_full, feed_at, feed_width, 0)
     weight_grads = (grad_queryw, grad_keyvalw, grad_outw, grad_upw, grad_down)
     summed = (
-        lax.psum(weight_grads[0].astype(jnp.bfloat16), "ctx").astype(jnp.float32),
+        jnp.sum(lax.all_gather(weight_grads[0].astype(jnp.bfloat16), "ctx"), axis=0).astype(
+            jnp.float32
+        ),
         lax.psum(weight_grads[1].astype(jnp.bfloat16), "ctx").astype(jnp.float32),
         lax.psum(weight_grads[2].astype(jnp.bfloat16), "ctx").astype(jnp.float32),
         lax.psum(weight_grads[3].astype(jnp.bfloat16), "ctx").astype(jnp.float32),

time: 824 us -> 890 us (1.080)
  waiting for transfers between devices: 372 us -> 434 us
    all_gather x0 -> x1, waiting for transfers between devices: none -> 91.5 us  [per_device(): lax.all_gather(weight_grads[0].astype(jnp.bfloat16), 'ctx')]
    psum x1, waiting for transfers between devices: 77.6 us -> 43.7 us  [per_device(): lax.psum(weight_grads[1].astype(jnp.bfloat16), 'ctx').astype(jnp.float32)]
    reduce_scatter x1, waiting for transfers between devices: 28.3 us -> 47.6 us  [per_device(): lax.psum_scatter(grad_kv_heads.astype(jnp.bfloat16), 'ctx', scatter_dimen...]
    unnamed x19 -> x20, waiting for transfers between devices: 51 us -> 36.5 us
    unnamed x108 -> x106, local copies, waits for them, and re-layouts: 38.4 us -> 36.7 us
  transfers between devices with their start and end apart: 15 -> 16, of which waited for: 12 -> 13; matrix products, arithmetic and copies ran while one was open for 14% -> 14% of each run, Pallas kernels for 0% -> 0%
where the time goes in v1:
time: 890 us; the launch traced here: 881 us
  waiting for transfers between devices  434 us (49%)
  matrix products  212 us (24%)
  blocking collectives  86 us (10%)
  other arithmetic  68.5 us (8%)
  local copies, waits for them, and re-layouts  64.2 us (7%)
  between operations  14.7 us (2%)
    all_gather x1, waiting for transfers between devices, per_device(): lax.all_gather(weight_grads[0].astype(jnp.bfloat16), 'ctx')  91.5 us
    reduce_scatter x1, waiting for transfers between devices, per_device(): lax.psum_scatter(grad_kv_heads.astype(jnp.bfloat16), 'ctx', scatter_dimen...  47.6 us
    psum x1, waiting for transfers between devices, per_device(): lax.psum(weight_grads[1].astype(jnp.bfloat16), 'ctx').astype(jnp.float32)  43.7 us
    psum x1, waiting for transfers between devices, per_device(): lax.psum(up_terms.astype(jnp.bfloat16), 'tp').astype(jnp.float32)  42.8 us
    psum x1, blocking collectives, per_device(): lax.psum((jnp.sum(grad_first_own * first_hat_own, axis=0), jnp.sum(grad_f...  42.3 us
    psum x1, waiting for transfers between devices, per_device(): lax.psum(down_terms.astype(jnp.bfloat16), 'tp').astype(jnp.float32)  41.2 us
    psum x1, waiting for transfers between devices, per_device(): lax.psum(attn_terms.astype(jnp.bfloat16), 'tp').astype(jnp.float32)  39.8 us
    unnamed x106, local copies, waits for them, and re-layouts  36.7 us
  transfers between devices with their start and end apart: 16, of which 13 were waited for; matrix products, arithmetic and copies ran while one was open for 14% of the time, Pallas kernels for 0%

profile of v1, /device:TPU:0, one launch (start us, length us, event | category | flops | bytes accessed | tf_op | source)
XLA Modules:
  0.0 881.3 jit_solution(2027505078301370303)
XLA Ops:
  8.6 10.9 %all_gather.32 = bf16[2,768,192]{1,2,0:T(8,128)(2,1)S(1)} all-gather(bf16[2,384,192]{1,2,0:T(8,128)(2,1)} %param.26), channel_id=1, replica_groups=mesh['shard'=2,'ctx'=4,'tp'=4] {'shard'}, dimensions={1}, use_global_device_ids=true | all-gather | bytes 884736 | tf_op jit(solution)/shard_map/all_gather | solution.py:77
  24.4 13.6 %all_gather.30 = s32[4,1024]{1,0:T(4,128)S(1)} all-gather(s32[4,256]{1,0:T(4,128)S(1)} %copy-done.42), channel_id=1, replica_groups=mesh['shard'=2,'ctx'=4,'tp'=4] {'ctx'}, dimensions={1}, use_global_device_ids=true | all-gather | bytes 20480 | tf_op jit(solution)/shard_map/all_gather | solution.py:113
  38.1 13.3 %all_gather.34 = s32[4,1024]{1,0:T(4,128)S(1)} all-gather(s32[4,256]{1,0:T(4,128)S(1)} %copy-done.21), channel_id=1, replica_groups=mesh['shard'=2,'ctx'=4,'tp'=4] {'ctx'}, dimensions={1}, use_global_device_ids=true | all-gather | bytes 20480 | tf_op jit(solution)/shard_map/all_gather | solution.py:114
  51.3 5.9 all_gather.35
  58.4 2.7 add_bitcast_fusion
  64.9 35.8 %all-gather.9.cloned.1.call-done = bf16[3,2,4,1024,64]{3,4,2,1,0:T(8,128)(2,1)} async-done(((bf16[3,2,4,256,64]{3,4,2,1,0:T(8,128)(2,1)}), bf16[3,2,4,1024,64]{3,4,2,1,0:T(8,128)(2,1)}) %all-gather.9.cloned.1.call-update) | async-done | bytes 3145744 | tf_op jit(solution)/shard_map/all_gather | solution.py:111
  100.7 30.9 %while.28 = (s32[]{:T(128)}, bf16[3,4,256,64]{2,3,1,0:T(8,128)(2,1)}, f32[3,4,256,1]{2,1,3,0:T(4,128)}, f32[3,4,256,1]{2,1,3,0:T(4,128)}, pred[4,1,1024]{2,0,1:T...) while((s32[]{:T(128)}, ...), condition=%wide.region_3.4_spmd.clone, body=%wide.region_0.3_spmd.clone.sunk | while | flops 420544512 | bytes 23113960 | solution.py:131
  102.5 2.8 select_reduce_fusion.2
  107.1 3.3 fusion.170
  112.8 2.8 select_reduce_fusion.2
  117.4 3.3 fusion.170
  123.1 2.8 select_reduce_fusion.2
  127.7 3.3 fusion.170
  136.4 39.8 %all-reduce.9.cloned.1.call-done = bf16[1024,768]{1,0:T(8,128)(2,1)} async-done(((bf16[1024,768]{1,0:T(8,128)(2,1)}), bf16[1024,768]{1,0:T(8,128)(2,1)}) %all-reduce.9.cloned.1.call-update) | async-done | bytes 1572880 | tf_op jit(solution)/shard_map/psum | solution.py:135
  181.4 19.1 %all-gather.11.cloned.1.call-done = bf16[768,768]{1,0:T(8,128)(2,1)} async-done(((bf16[384,768]{1,0:T(8,128)(2,1)}), bf16[768,768]{1,0:T(8,128)(2,1)}) %all-gather.11.cloned.1.call-update) | async-done | bytes 1179664 | tf_op jit(solution)/shard_map/all_gather | solution.py:79
  200.5 10.3 %fusion.93 = (bf16[1024,768]{1,0:T(8,128)(2,1)}, f32[1024,768]{1,0:T(8,128)}) fusion(f32[768]{0:T(1024)S(1)} %copy-done.49, bf16[768,768]{1,0:T(8,128)(2,1)} %all-gather.11.cloned.1.call-done, f32[1024,768]{1,0:T(8,128)S(1)} %subtract_multiply_fusion.3, f32[768]{0:T(1024)S(1)} %copy-done.35, f32[768]{0:T(1024)S(1)} %copy-done.28), kind=kOutput, calls=%fused_computation.90 | convolution fusion | flops 1262223360 | bytes 9053184 | tf_op jit(solution)/shard_map/dot_general | solution.py:140
  210.8 13.9 %all-gather.13.cloned.1.call-done = bf16[768,768]{1,0:T(8,128)(2,1)} async-done(((bf16[768,384]{1,0:T(8,128)(2,1)}), bf16[768,768]{1,0:T(8,128)(2,1)}) %all-gather.13.cloned.1.call-update) | async-done | bytes 1179664 | tf_op jit(solution)/shard_map/all_gather | solution.py:80
  224.7 4.3 convolution_convert_fusion.1
  230.8 41.2 %all-reduce.11.cloned.1.call-done = bf16[1024,768]{1,0:T(8,128)(2,1)} async-done(((bf16[1024,768]{1,0:T(8,128)(2,1)}), bf16[1024,768]{1,0:T(8,128)(2,1)}) %all-reduce.11.cloned.1.call-update) | async-done | bytes 1572880 | tf_op jit(solution)/shard_map/psum | solution.py:149
  281.3 3.4 convert_reduce_fusion
  288.8 42.8 %all-reduce.13.cloned.1.call-done = bf16[1024,768]{1,0:T(8,128)(2,1)} async-done(((bf16[1024,768]{1,0:T(8,128)(2,1)}), bf16[1024,768]{1,0:T(8,128)(2,1)}) %all-reduce.13.cloned.1.call-update) | async-done | bytes 1572880 | tf_op jit(solution)/shard_map/psum | solution.py:161
  331.6 4.8 multiply_reduce_fusion.6
  343.8 150.2 %while.29 = (s32[]{:T(128)}, bf16[3,2,4,256,64]{3,4,2,1,0:T(8,128)(2,1)}, bf16[3,2,4,1024,64]{3,4,2,1,0:T(8,128)(2,1)}, pred[4,1,1024]{2,0,1:T(4,128)(4,1)}, bf1...) while((s32[]{:T(128)}, ...), condition=%wide.region_17.18_spmd.clone, body=%wide.region_15.17_spmd.clone.sunk | while | flops 1123033088 | bytes 97640736 | solution.py:213
  344.5 3.8 fusion.179
  350.1 5.0 exponential_divide_fusion.2
  355.2 7.7 fusion.181
  362.9 7.7 fusion.180
  372.3 3.5 fusion.183
  375.7 7.9 fusion.184
  383.6 8.0 fusion.185
  394.5 3.8 fusion.179
  400.2 5.0 exponential_divide_fusion.2
  405.2 7.7 fusion.181
  412.9 7.7 fusion.180
  422.3 3.5 fusion.183
  425.8 7.9 fusion.184
  433.7 8.0 fusion.185
  444.6 3.8 fusion.179
  450.2 5.0 exponential_divide_fusion.2
  455.3 7.7 fusion.181
  463.0 7.7 fusion.180
  472.4 3.5 fusion.183
  475.9 7.9 fusion.184
  483.7 8.0 fusion.185
  499.9 4.6 convolution_convert_fusion.3
  506.9 47.6 %reduce-scatter.15.cloned.1.call-done = bf16[3,2,4,256,64]{3,4,2,1,0:T(8,128)(2,1)} async-done(((bf16[3,2,4,1024,64]{3,4,2,1,0:T(8,128)(2,1)}), bf16[3,2,4,256,64]{3,4,2,1,0:T(8,128)(2,1)}) %reduce-scatter.15.cloned.1.call-update) | async-done | bytes 786448 | tf_op jit(solution)/shard_map/reduce_scatter | solution.py:216
  554.6 2.6 copy.55
  559.7 3.3 fusion.112
  563.0 3.0 copy.58
  566.0 3.0 reshape.230
  569.1 3.9 convolution_convert_fusion.4
  581.0 3.8 fusion.110
  584.9 3.2 fusion.120
  596.6 15.5 %reduce-scatter.21.cloned.1.call-done = bf16[384,384]{1,0:T(8,128)(2,1)} async-done(((bf16[768,384]{1,0:T(8,128)(2,1)}), bf16[384,384]{1,0:T(8,128)(2,1)}) %reduce-scatter.21.cloned.1.call-update) | async-done | bytes 294928
  614.6 22.1 %reduce-scatter.17.cloned.1.call-done = bf16[384,768]{1,0:T(8,128)(2,1)} async-done(((bf16[768,768]{1,0:T(8,128)(2,1)}), bf16[384,768]{1,0:T(8,128)(2,1)}) %reduce-scatter.17.cloned.1.call-update) | async-done | bytes 589840 | tf_op jit(solution)/shard_map/reduce_scatter | solution.py:295
  636.8 91.5 %all-gather.15.cloned.1.call-done = bf16[16,768,192]{1,2,0:T(8,128)(2,1)} async-done(((bf16[4,768,192]{1,2,0:T(8,128)(2,1)}), bf16[16,768,192]{1,2,0:T(8,128)(2,1)}) %all-gather.15.cloned.1.call-update) | async-done | bytes 4718608 | tf_op jit(solution)/shard_map/all_gather | solution.py:277
  728.3 4.4 reduce_sum.193
  732.6 3.6 copy.56
  736.3 4.0 reshape.228
  740.3 3.4 bitcast_convert_fusion
  754.6 42.3 %all-reduce.1 = (f32[4,768]{1,0:T(4,128)S(1)}, f32[768]{0:T(1024)S(1)}, f32[768]{0:T(1024)}, f32[768]{0:T(1024)}, f32[768]{0:T(1024)}, /*index=5*/f32[3072]{0:T(...) all-reduce(f32[4,768]{1,0:T(4,128)S(1)} %dynamic_update_slice.28, ...), channel_id=1, replica_groups=mesh['shard'=2,'ctx'=4,'tp'=4] {'shard','ctx','tp'}, use_global_device_ids=true, to_apply=%region_25.26 | all-reduce | flops 11520 | bytes 92160 | tf_op jit(solution)/shard_map/psum | solution.py:247
  798.9 4.1 convert_add_fusion
  803.0 43.7 %all-reduce.17.cloned.1.call-done = (bf16[2,384,192]{1,2,0:T(8,128)(2,1)}, bf16[192,384]{1,0:T(8,128)(2,1)}, bf16[384,768]{1,0:T(8,128)(2,1)}, bf16[768,384]{1,0:T(8,128)(2,1)}) async-done(((bf16[2,384,192]{1,2,0:T(8,128)(2,1)}, bf16[192,384]{1,0:T(8,128)(2,1)}, bf16[384,768]{1,0:T(8,128)(2,1)}, bf16[768,384]{1,0:T(8,128)(2,1)}), (bf16[2,384,192]{1,2,0:T(8,128)(2,1)}, bf16[192,384]{1,0:T(8,128)(2,1)}, ...) | async-done | bytes 1622032 | tf_op jit(solution)/shard_map/psum | solution.py:280
  853.5 16.8 %reduce-scatter.19.cloned.1.call-done = bf16[384,768]{1,0:T(8,128)(2,1)} async-done(((bf16[768,768]{1,0:T(8,128)(2,1)}), bf16[384,768]{1,0:T(8,128)(2,1)}) %reduce-scatter.19.cloned.1.call-update) | async-done | bytes 589840
  (268 shorter events, 129.5 us)
Async XLA Ops:
  7.2 51.2 %all-gather.7.cloned.1.call-start = ((), (), s32[]{:S(2)}) async-start(), calls=%async_computation.6 | async-start | bytes 1769472 | tf_op jit(solution)/shard_map/all_gather | solution.py:76
  7.9 92.7 %all-gather.9.cloned.1.call-start = ((), (), s32[]{:S(2)}) async-start(), calls=%async_computation.7 | async-start | bytes 3932160 | tf_op jit(solution)/shard_map/all_gather | solution.py:111
  20.4 4.0 copy-start.42
  20.4 17.7 %copy-start.21 = (s32[4,256]{1,0:T(4,128)S(1)}, s32[4,256]{1,0:T(4,128)}, u32[]{:S(2)}) copy-start(s32[4,256]{1,0:T(4,128)} %param.24) | copy-start | bytes 12292
  20.4 31.0 %copy-start.30 = (bf16[192,384]{1,0:T(8,128)(2,1)S(1)}, bf16[192,384]{1,0:T(8,128)(2,1)}, u32[]{:S(2)}) copy-start(bf16[192,384]{1,0:T(8,128)(2,1)} %param.29) | copy-start | bytes 442372
  22.6 35.8 %copy-start.3 = (bf16[4,256,768]{2,1,0:T(8,128)(2,1)S(1)}, bf16[4,256,768]{2,1,0:T(8,128)(2,1)}, u32[]{:S(2)}) copy-start(bf16[4,256,768]{2,1,0:T(8,128)(2,1)} %param.22) | copy-start | bytes 4718596
  22.7 35.8 %copy-start.48 = (f32[4,192]{1,0:T(4,128)S(1)}, f32[4,192]{1,0:T(4,128)}, u32[]{:S(2)}) copy-start(f32[4,192]{1,0:T(4,128)} %param.27) | copy-start | bytes 9220
  24.3 151.9 %all-reduce.9.cloned.1.call-start = ((), (), s32[]{:S(2)}) async-start(), calls=%async_computation.8 | async-start | bytes 3145728 | tf_op jit(solution)/shard_map/psum | solution.py:135
  24.4 36.7 %copy-start.43 = (pred[1024]{0:T(1024)(128)(4,1)}, pred[1024]{0:T(1024)(128)(4,1)S(1)}, u32[]{:S(2)}) copy-start(pred[1024]{0:T(1024)(128)(4,1)S(1)} %eq.36) | copy-start | bytes 3076
  100.7 32.6 %copy-start.19 = (bf16[192,768]{1,0:T(8,128)(2,1)S(1)}, bf16[192,768]{1,0:T(8,128)(2,1)}, u32[]{:S(2)}) copy-start(bf16[192,768]{1,0:T(8,128)(2,1)} %all_gather.35) | copy-start | bytes 884740
  100.7 1.9 copy-start.24
  100.7 1.9 copy-start.26
  111.0 1.8 copy-start.24
  111.0 1.9 copy-start.26
  121.3 1.8 copy-start.26
  131.6 4.7 copy-start.6
  131.6 44.7 %copy-start.41 = (f32[768]{0:T(1024)S(1)}, f32[768]{0:T(1024)}, u32[]{:S(2)}) copy-start(f32[768]{0:T(1024)} %param.30) | copy-start | bytes 9220
  133.2 45.1 %copy-start.8 = (bf16[24,8,4,256]{3,1,2,0:T(8,128)(2,1)}, bf16[24,8,4,256]{3,1,2,0:T(8,128)(2,1)S(1)}, u32[]{:S(2)}) copy-start(bf16[24,8,4,256]{3,1,2,0:T(8,128)(2,1)S(1)} %copy.64) | copy-start | bytes 1179652
  135.0 65.4 %all-gather.11.cloned.1.call-start = ((), (), s32[]{:S(2)}) async-start(), calls=%async_computation.9 | async-start | bytes 1769472 | tf_op jit(solution)/shard_map/all_gather | solution.py:79
  135.6 89.0 %all-gather.13.cloned.1.call-start = ((), (), s32[]{:S(2)}) async-start(), calls=%async_computation.10 | async-start | bytes 1769472 | tf_op jit(solution)/shard_map/all_gather | solution.py:80
  136.2 135.8 %all-reduce.11.cloned.1.call-start = ((), (), s32[]{:S(2)}) async-start(), calls=%async_computation.11 | async-start | bytes 3145728 | tf_op jit(solution)/shard_map/psum | solution.py:149
  176.2 2.1 copy-start.4
  179.3 157.1 %copy-start.32 = (f32[1024]{0:T(1024)}, f32[1024]{0:T(1024)S(1)}, u32[]{:S(2)}) copy-start(f32[1024]{0:T(1024)S(1)} %add_rsqrt_fusion.1) | copy-start | bytes 12292
  179.3 21.2 %copy-start.28 = (f32[768]{0:T(1024)S(1)}, f32[768]{0:T(1024)}, u32[]{:S(2)}) copy-start(f32[768]{0:T(1024)} %param.31) | copy-start | bytes 9220
  179.3 21.2 %copy-start.35 = (f32[768]{0:T(1024)S(1)}, f32[768]{0:T(1024)}, u32[]{:S(2)}) copy-start(f32[768]{0:T(1024)} %param.32) | copy-start | bytes 9220
  179.3 21.2 %copy-start.49 = (f32[768]{0:T(1024)S(1)}, f32[768]{0:T(1024)}, u32[]{:S(2)}) copy-start(f32[768]{0:T(1024)} %param.34) | copy-start | bytes 9220
  224.7 4.4 copy-start.31
  228.9 43.1 %copy-start.34 = (f32[768]{0:T(1024)S(1)}, f32[768]{0:T(1024)}, u32[]{:S(2)}) copy-start(f32[768]{0:T(1024)} %param.36) | copy-start | bytes 9220
  229.0 102.6 %all-reduce.13.cloned.1.call-start = ((), (), s32[]{:S(2)}) async-start(), calls=%async_computation.12 | async-start | bytes 3145728 | tf_op jit(solution)/shard_map/psum | solution.py:161
  272.0 2.2 copy-start.5
  277.4 2.2 copy-start.47
  277.4 3.9 copy-start.51
  279.1 5.7 copy-start.11
  281.3 4.6 copy-start.46
  285.9 45.7 %copy-start.45 = (f32[768]{0:T(1024)S(1)}, f32[768]{0:T(1024)}, u32[]{:S(2)}) copy-start(f32[768]{0:T(1024)} %param.38) | copy-start | bytes 9220
  288.5 266.1 %reduce-scatter.15.cloned.1.call-start = ((), (), s32[]{:S(2)}) async-start(), calls=%async_computation.13 | async-start | bytes 3932160 | tf_op jit(solution)/shard_map/reduce_scatter | solution.py:216
  348.2 1.9 copy-start.23
  348.2 1.9 copy-start.25
  348.2 1.9 copy-start.27
  398.3 1.9 copy-start.23
  398.3 1.9 copy-start.25
  398.3 1.9 copy-start.27
  448.3 1.9 copy-start.23
  448.3 1.9 copy-start.25
  448.3 1.9 copy-start.27
  494.0 96.6 %reduce-scatter.23.cloned.1.call-start = ((), (), s32[]{:S(2)}) async-start(), calls=%async_computation.19 | async-start | bytes 589824
  499.4 95.0 %reduce-scatter.25.cloned.1.call-start = ((), (), s32[]{:S(2)}) async-start(), calls=%async_computation.20 | async-start | bytes 1769472
  506.9 105.3 %reduce-scatter.21.cloned.1.call-start = ((), (), s32[]{:S(2)}) async-start(), calls=%async_computation.18 | async-start | bytes 884736
  559.7 9.4 %copy-start.29 = (f32[768]{0:T(1024)S(1)}, f32[768]{0:T(1024)}, u32[]{:S(2)}) copy-start(f32[768]{0:T(1024)} %param.31) | copy-start | bytes 9220
  559.7 9.4 %copy-start.36 = (f32[768]{0:T(1024)S(1)}, f32[768]{0:T(1024)}, u32[]{:S(2)}) copy-start(f32[768]{0:T(1024)} %param.32) | copy-start | bytes 9220
  569.0 67.7 %reduce-scatter.17.cloned.1.call-start = ((), (), s32[]{:S(2)}) async-start(), calls=%async_computation.16 | async-start | bytes 1769472 | tf_op jit(solution)/shard_map/reduce_scatter | solution.py:295
  573.0 5.7 copy-start.44
  573.0 155.3 %all-gather.15.cloned.1.call-start = ((), (), s32[]{:S(2)}) async-start(), calls=%async_computation.15 | async-start | bytes 5898240 | tf_op jit(solution)/shard_map/all_gather | solution.py:277
  579.9 5.0 copy-start.14
  584.8 214.1 %all-reduce.15.cloned.1.call-start = ((), (), s32[]{:S(2)}) async-start(), calls=%async_computation.14 | async-start | bytes 3145728 | tf_op jit(solution)/shard_map/psum | solution.py:243
  584.9 3.2 copy-start.10
  584.9 3.2 copy-start.13
  590.4 256.4 %all-reduce.17.cloned.1.call-start = ((), (), s32[]{:S(2)}) async-start(), calls=%async_computation.21 | async-start | bytes 3244032 | tf_op jit(solution)/shard_map/psum | solution.py:280
  636.7 233.5 %reduce-scatter.19.cloned.1.call-start = ((), (), s32[]{:S(2)}) async-start(), calls=%async_computation.17 | async-start | bytes 1769472
  740.3 7.7 copy-start.15
  743.7 55.2 %copy-start.33 = (f32[1024]{0:T(1024)S(1)}, f32[1024]{0:T(1024)}, u32[]{:S(2)}) copy-start(f32[1024]{0:T(1024)} %copy-done.32) | copy-start | bytes 12292
  743.7 55.2 %copy-start.38 = (f32[1024]{0:T(1024)S(1)}, f32[1024]{0:T(1024)}, u32[]{:S(2)}) copy-start(f32[1024]{0:T(1024)} %copy-done.37) | copy-start | bytes 12292
  743.7 55.2 %copy-start.40 = (f32[1024]{0:T(1024)S(1)}, f32[1024]{0:T(1024)}, u32[]{:S(2)}) copy-start(f32[1024]{0:T(1024)} %copy-done.39) | copy-start | bytes 12292
  846.7 5.7 copy-start.20
  (16 other events, 22.6 us)
Sparse Core Ops, SparseCore 0:
  9.5 25.4 all-gather.6
  37.2 63.4 all-gather.8
  135.2 41.0 all-reduce.8
  177.6 22.7 all-gather.10
  201.9 22.7 all-gather.12
  229.1 42.8 all-reduce.10
  288.6 42.8 all-reduce.12
  494.1 60.4 reduce-scatter.14
  556.8 13.1 reduce-scatter.22
  572.6 21.8 reduce-scatter.24
  596.7 15.3 reduce-scatter.20
  614.8 21.8 reduce-scatter.16
  638.8 89.3 all-gather.14
  730.5 41.9 all-reduce.14
  775.6 71.0 all-reduce.16
  849.4 20.8 reduce-scatter.18
